TPU v7x, 256 devices: a whole 4x4x8 slice. The times are simulated.
256 devices in a mesh: dp: 2 (over y_hi), fsdp: 16 (over x, y_lo, core), tensor: 8 (over z).
Axes of the slice: x: 4, y: 4 (y_hi: 2, y_lo: 2; y = y_hi * 2 + y_lo), z: 8, core: 2. Of those that a mesh axis runs over, the one named last changes fastest.
Arguments:
- activations: bfloat16 [4096, 8192], P(('dp', 'fsdp'), 'tensor'), may hold values from -6 to 6
- cotangent: bfloat16 [4096, 8192], P(('dp', 'fsdp'), 'tensor'), may hold values from -6 to 6
- up_tiles: bfloat16 [1024, 128, 128], P(('fsdp', 'tensor')), may hold values from -0.1875 to 0.1875
- down_tiles: bfloat16 [1024, 128, 128], P(('fsdp', 'tensor')), may hold values from -0.125 to 0.125
- up_rows: int32 [128, 8], P(None, 'tensor'), may hold values from 0 to 63, as said below
- up_cols: int32 [128, 8], P(None, 'tensor'), may hold values from 0 to 15, as said below
- down_rows: int32 [128, 8], P(None, 'tensor'), may hold values from 0 to 15, as said below
- down_cols: int32 [128, 8], P(None, 'tensor'), may hold values from 0 to 63, as said below
Outputs:
- output: bfloat16 [4096, 8192], P(('dp', 'fsdp'), 'tensor')
- input_grad: bfloat16 [4096, 8192], P(('dp', 'fsdp'), 'tensor')
- up_grad: float32 [1024, 128, 128], P(('fsdp', 'tensor'))
- down_grad: float32 [1024, 128, 128], P(('fsdp', 'tensor'))
Inputs may be any that keep to these rules, and one draw needn't show every extreme that they name: `up_rows`: within a column, the up tiles of one hidden-unit block name distinct feature blocks. `up_cols`: every value occurs exactly 8 times in each column. `down_rows`: every value occurs exactly 8 times in each column. `down_cols`: within a column, the down tiles of one hidden-unit block name distinct feature blocks.
All inputs are finite; a program needn't handle non-finite values.
Results may differ from a plain program's by a relative error of at most 0.018.
Values may be sent and summed in bfloat16 or wider, within the bound.
No kernel may reach another device: no remote copies, remote signals or barrier semaphores. Data moves between devices by JAX's collectives and lax.ppermute only.
A program may use at most 128 MiB of HBM per device.

v0:
```python
import jax
import jax.numpy as jnp
from jax import lax
from jax.sharding import PartitionSpec as P

D = 8192
FF = 16384
inv_root_two = 0.7071067811865476
inv_root_tau = 0.3989422804014327


def gelu_parts(values):
    normal_cdf = 0.5 * (1.0 + jax.scipy.special.erf(values * inv_root_two))
    density = inv_root_tau * jnp.exp(-0.5 * values * values)
    return (values * normal_cdf, normal_cdf + values * density)


def grouped_pick(acting, far_index, hidden_blocks, block_size):
    rows_here = acting.shape[0]
    picked = acting.reshape(rows_here, -1, block_size)[:, far_index]
    return picked.reshape(rows_here, hidden_blocks, -1, block_size)


def add_far(product, far_index, model_blocks):
    rows_here = product.shape[0]
    block_size = product.shape[-1]
    flat = product.reshape(rows_here, -1, block_size)
    summed = (
        jnp.zeros((rows_here, model_blocks, block_size), jnp.float32).at[:, far_index].add(flat)
    )
    return summed.reshape(rows_here, model_blocks * block_size)


def grouped_tiles(tiles, order, hidden_blocks):
    block_size = tiles.shape[1]
    return tiles[order].reshape(hidden_blocks, -1, block_size, block_size)


def body(activations, cotangent, up_tiles, down_tiles, up_rows, up_cols, down_rows, down_cols):
    block_size = up_tiles.shape[1]
    hidden_blocks = FF // (block_size * lax.axis_size("tensor"))
    model_blocks = D // block_size
    up_order = jnp.argsort(up_cols[:, 0], stable=True)
    down_order = jnp.argsort(down_rows[:, 0], stable=True)
    up_back = jnp.argsort(up_order)
    down_back = jnp.argsort(down_order)
    up_far = up_rows[:, 0][up_order]
    down_far = down_cols[:, 0][down_order]
    full_input = lax.all_gather(activations, "tensor", axis=1, tiled=True)
    input_pick = grouped_pick(full_input, up_far, hidden_blocks, block_size)
    up_whole = lax.all_gather(up_tiles, "fsdp", axis=0, tiled=True)
    up_sorted = grouped_tiles(up_whole, up_order, hidden_blocks)
    pre_act = jnp.einsum(
        "thkb,hkbc->thc", input_pick, up_sorted, preferred_element_type=jnp.float32
    )
    gelu_out, gelu_slope = gelu_parts(pre_act)
    hidden = gelu_out.astype(jnp.bfloat16)
    down_whole = lax.all_gather(down_tiles, "fsdp", axis=0, tiled=True)
    down_sorted = grouped_tiles(down_whole, down_order, hidden_blocks)
    out_product = jnp.einsum(
        "thb,hkbc->thkc", hidden, down_sorted, preferred_element_type=jnp.float32
    )
    partial_out = add_far(out_product, down_far, model_blocks)
    output = lax.psum_scatter(
        partial_out.astype(jnp.bfloat16), "tensor", scatter_dimension=1, tiled=True
    )
    full_cotangent = lax.all_gather(cotangent, "tensor", axis=1, tiled=True)
    cot_pick = grouped_pick(full_cotangent, down_far, hidden_blocks, block_size)
    hidden_grad = jnp.einsum(
        "thkc,hkbc->thb", cot_pick, down_sorted, preferred_element_type=jnp.float32
    )
    pre_grad = (hidden_grad * gelu_slope).astype(jnp.bfloat16)
    in_product = jnp.einsum(
        "thc,hkbc->thkb", pre_grad, up_sorted, preferred_element_type=jnp.float32
    )
    partial_in = add_far(in_product, up_far, model_blocks)
    input_grad = lax.psum_scatter(
        partial_in.astype(jnp.bfloat16), "tensor", scatter_dimension=1, tiled=True
    )
    up_grouped = jnp.einsum(
        "thkb,thc->hkbc", input_pick, pre_grad, preferred_element_type=jnp.float32
    )
    down_grouped = jnp.einsum(
        "thb,thkc->hkbc", hidden, cot_pick, preferred_element_type=jnp.float32
    )
    up_rounded = up_grouped.astype(jnp.bfloat16).reshape(-1, block_size, block_size)
    down_rounded = down_grouped.astype(jnp.bfloat16).reshape(-1, block_size, block_size)
    up_term = up_rounded[up_back].astype(jnp.float32)
    down_term = down_rounded[down_back].astype(jnp.float32)
    up_part, down_part = (
        lax.psum_scatter(
            up_term.astype(jnp.bfloat16), "fsdp", scatter_dimension=0, tiled=True
        ).astype(jnp.float32),
        lax.psum_scatter(
            down_term.astype(jnp.bfloat16), "fsdp", scatter_dimension=0, tiled=True
        ).astype(jnp.float32),
    )
    up_grad, down_grad = (
        lax.psum(up_part.astype(jnp.bfloat16), "dp").astype(jnp.float32),
        lax.psum(down_part.astype(jnp.bfloat16), "dp").astype(jnp.float32),
    )
    return (output, input_grad, up_grad, down_grad)


def solution(mesh):
    in_specs = (
        P(("dp", "fsdp"), "tensor"),
        P(("dp", "fsdp"), "tensor"),
        P(("fsdp", "tensor"), None, None),
        P(("fsdp", "tensor"), None, None),
        P(None, "tensor"),
        P(None, "tensor"),
        P(None, "tensor"),
        P(None, "tensor"),
    )
    out_specs = (
        P(("dp", "fsdp"), "tensor"),
        P(("dp", "fsdp"), "tensor"),
        P(("fsdp", "tensor"), None, None),
        P(("fsdp", "tensor"), None, None),
    )
    return jax.shard_map(body, mesh=mesh, in_specs=in_specs, out_specs=out_specs, check_vma=False)
```

profile of v0, /device:TPU:1, one launch (start us, length us, event | category | flops | bytes accessed | tf_op | source)
XLA Modules:
  0.0 480.6 jit_solution(9236470539080875752)
XLA Ops:
  7.2 1.8 copy.58
  9.1 1.8 copy.65
  11.0 0.7 all-gather.7.cloned.1.call-update
  11.7 0.5 all-gather.5.cloned.1.call-update
  12.3 3.2 sort.63
  15.5 2.5 sort.64
  18.0 1.2 gather_fusion.3
  19.3 3.2 sort.62
  22.5 1.6 gather_fusion
  24.1 28.0 %all-gather.9.cloned.1.call-done = bf16[128,8192]{0,1:T(8,128)(2,1)} async-done(((bf16[128,1024]{0,1:T(8,128)(2,1)}), bf16[128,8192]{0,1:T(8,128)(2,1)}) %all-gather.9.cloned.1.call-update) | async-done | bytes 2097168 | tf_op jit(solution)/shard_map/all_gather | solution.py:49
  52.1 3.2 copy.59
  55.3 39.0 %all-gather.11.cloned.1.call-done = bf16[128,8192]{0,1:T(8,128)(2,1)} async-done(((bf16[128,1024]{0,1:T(8,128)(2,1)}), bf16[128,8192]{0,1:T(8,128)(2,1)}) %all-gather.11.cloned.1.call-update) | async-done | bytes 2097168 | tf_op jit(solution)/shard_map/all_gather | solution.py:67
  94.3 4.1 copy.66
  98.4 3.0 gather_fusion.4
  101.4 4.6 gather_fusion.5
  106.0 32.7 %all-gather.7.cloned.1.call-done = bf16[128,128,128]{2,1,0:T(8,128)(2,1)} async-done(((bf16[8,128,128]{2,1,0:T(8,128)(2,1)}), bf16[128,128,128]{2,1,0:T(8,128)(2,1)}) %all-gather.7.cloned.1.call-update) | async-done | bytes 4194320 | tf_op jit(solution)/shard_map/all_gather | solution.py:51
  138.7 5.2 %gather_fusion.2 = bf16[128,128,128]{2,1,0:T(8,128)(2,1)} fusion(bf16[128,128,128]{2,1,0:T(8,128)(2,1)} %all-gather.7.cloned.1.call-done, s32[1024]{0:T(1024)S(1)} %pad_clamp_fusion.4), kind=kCustom, calls=%fused_computation.2 | custom fusion | bytes 8389120 | tf_op jit(solution)/shard_map/gather | solution.py:36
  143.9 4.8 convolution_bitcast_fusion.1
  148.7 31.7 %all-gather.5.cloned.1.call-done = bf16[128,128,128]{2,1,0:T(8,128)(2,1)} async-done(((bf16[8,128,128]{2,1,0:T(8,128)(2,1)}), bf16[128,128,128]{2,1,0:T(8,128)(2,1)}) %all-gather.5.cloned.1.call-update) | async-done | bytes 4194320 | tf_op jit(solution)/shard_map/all_gather | solution.py:58
  180.5 5.2 %gather_fusion.1 = bf16[128,128,128]{2,1,0:T(8,128)(2,1)} fusion(bf16[128,128,128]{2,1,0:T(8,128)(2,1)} %all-gather.5.cloned.1.call-done, s32[1024]{0:T(1024)S(1)} %pad_clamp_fusion.5), kind=kCustom, calls=%fused_computation.1 | custom fusion | bytes 8389120 | tf_op jit(solution)/shard_map/gather | solution.py:36
  185.7 5.0 %fusion.2 = bf16[128,16,128,1]{0,2,3,1:T(8,128)(2,1)S(1)} fusion(bf16[16,8,128,128]{3,2,1,0:T(8,128)(2,1)} %bitcast.84, bf16[128,16,8,128]{3,0,2,1:T(8,128)(2,1)} %bitcast.86, f32[128,16,128]{0,2,1:T(8,128)S(1)} %convolution_bitcast_fusion.1), kind=kOutput, calls=%fused_computation.17 | convolution fusion | flops 539492352 | bytes 9961472 | tf_op jit(solution)/shard_map/thkc,hkbc->thb/dot_general | solution.py:69
  190.7 3.3 convolution_convert_fusion.1
  194.0 5.2 %gather_fusion.6 = bf16[128,128,128]{2,1,0:T(8,128)(2,1)} fusion(bf16[128,128,128]{2,1,0:T(8,128)(2,1)} %bitcast.88, s32[1024]{0:T(1024)S(1)} %pad_clamp_fusion.1), kind=kCustom, calls=%fused_computation.6 | custom fusion | bytes 8389120 | tf_op jit(solution)/shard_map/gather | solution.py:88
  199.2 0.2 reduce-scatter.11.cloned.1.call-start
  199.5 2.5 sort.65
  202.0 5.6 %convolution_convert_fusion = bf16[16,8,128,128]{3,2,1,0:T(8,128)(2,1)} fusion(bf16[128,16,8,128]{3,0,2,1:T(8,128)(2,1)} %bitcast.87, f32[128,16,128]{0,2,1:T(8,128)S(1)} %convolution_bitcast_fusion.1), kind=kOutput, calls=%fused_computation.10 | convolution fusion | flops 540278784 | bytes 9437184 | tf_op jit(solution)/shard_map/thb,thkc->hkbc/dot_general | solution.py:83
  207.6 6.4 %copy.74 = bf16[128,128,128]{2,1,0:T(8,128)(2,1)} copy(bf16[128,128,128]{1,2,0:T(8,128)(2,1)} %bitcast.89) | data formatting | bytes 8388608 | tf_op jit(solution)/shard_map/reshape | solution.py:87
  214.0 5.3 %gather_fusion.7 = bf16[128,128,128]{2,1,0:T(8,128)(2,1)} fusion(bf16[128,128,128]{2,1,0:T(8,128)(2,1)} %copy.74, s32[1024]{0:T(1024)S(1)} %pad_clamp_fusion), kind=kCustom, calls=%fused_computation.7 | custom fusion | bytes 8389120 | tf_op jit(solution)/shard_map/gather | solution.py:89
  219.4 6.7 %fusion.13 = f32[16,8,128,128]{3,2,1,0:T(8,128)} fusion(bf16[16,8,128,128]{3,2,1,0:T(8,128)(2,1)} %bitcast.77, bf16[128,16,128,1]{0,2,3,1:T(8,128)(2,1)S(1)} %fusion.2), kind=kOutput, calls=%fused_computation.40 | convolution fusion | flops 536870912 | bytes 13107200 | tf_op jit(solution)/shard_map/thc,hkbc->thkb/dot_general | solution.py:73
  226.1 9.0 %copy.68 = f32[128,128,128]{2,0,1:T(8,128)} copy(f32[128,128,128]{0,2,1:T(8,128)} %bitcast.82) | data formatting | bytes 16777216 | tf_op jit(solution)/shard_map/reshape | solution.py:27
  235.1 2.5 broadcast.42.clone.1
  237.6 26.7 %scatter_fusion.1 = f32[128,64,128]{2,0,1:T(8,128)} fusion(f32[128,64,128]{2,0,1:T(8,128)} %broadcast.42.clone.1, s32[128]{0:T(128)S(1)} %fusion.9, f32[128,128,128]{2,1,0:T(8,128)} %bitcast.81), kind=kCustom, calls=%fused_computation.9 | custom fusion | flops 2097152 | bytes 25166336 | tf_op jit(solution)/shard_map/scatter-add | solution.py:29
  264.3 2.6 convert_element_type.45
  266.9 2.9 copy.69
  270.0 6.8 %fusion.11 = f32[16,8,128,128]{3,2,1,0:T(8,128)} fusion(bf16[16,8,128,128]{3,2,1,0:T(8,128)(2,1)} %bitcast.85, f32[128,16,128]{0,2,1:T(8,128)S(1)} %convolution_bitcast_fusion.1), kind=kOutput, calls=%fused_computation.39 | convolution fusion | flops 538181632 | bytes 13631488 | tf_op jit(solution)/shard_map/thb,hkbc->thkc/dot_general | solution.py:60
  276.7 9.0 %copy.63 = f32[128,128,128]{2,0,1:T(8,128)} copy(f32[128,128,128]{0,2,1:T(8,128)} %bitcast.83) | data formatting | bytes 16777216 | tf_op jit(solution)/shard_map/reshape | solution.py:27
  285.8 2.5 broadcast.42.clone
  288.2 26.9 %scatter_fusion = f32[128,64,128]{2,0,1:T(8,128)} fusion(f32[128,64,128]{2,0,1:T(8,128)} %broadcast.42.clone, s32[128]{0:T(128)S(1)} %fusion.8, f32[128,128,128]{2,1,0:T(8,128)} %bitcast.80), kind=kCustom, calls=%fused_computation.8 | custom fusion | flops 2097152 | bytes 25166336 | tf_op jit(solution)/shard_map/scatter-add | solution.py:29
  315.1 2.6 convert_element_type.42
  317.7 2.9 copy.64
  320.7 16.4 %reduce-scatter.11.cloned.1.call-done = bf16[8,128,128]{2,1,0:T(8,128)(2,1)} async-done(((bf16[128,128,128]{2,1,0:T(8,128)(2,1)}), bf16[8,128,128]{2,1,0:T(8,128)(2,1)}) %reduce-scatter.11.cloned.1.call-update) | async-done | bytes 262160 | tf_op jit(solution)/shard_map/reduce_scatter | solution.py:94
  337.1 42.2 %reduce-scatter.7.cloned.1.call-done = bf16[128,1024]{0,1:T(8,128)(2,1)} async-done(((bf16[128,8192]{0,1:T(8,128)(2,1)}), bf16[128,1024]{0,1:T(8,128)(2,1)}) %reduce-scatter.7.cloned.1.call-update) | async-done | bytes 262160 | tf_op jit(solution)/shard_map/reduce_scatter | solution.py:77
  379.4 1.8 copy.76
  381.1 41.9 %reduce-scatter.5.cloned.1.call-done = bf16[128,1024]{0,1:T(8,128)(2,1)} async-done(((bf16[128,8192]{0,1:T(8,128)(2,1)}), bf16[128,1024]{0,1:T(8,128)(2,1)}) %reduce-scatter.5.cloned.1.call-update) | async-done | bytes 262160 | tf_op jit(solution)/shard_map/reduce_scatter | solution.py:64
  423.0 1.8 copy.75
  424.8 45.7 %all-reduce.3.cloned.1.call-done = (bf16[8,128,128]{2,1,0:T(8,128)(2,1)}, bf16[8,128,128]{2,1,0:T(8,128)(2,1)}) async-done(((bf16[8,128,128]{2,1,0:T(8,128)(2,1)}, bf16[8,128,128]{2,1,0:T(8,128)(2,1)}), (bf16[8,128,128]{2,1,0:T(8,128)(2,1)}, bf16[8,128,128]{2,1,0:T(8,128)(2,1)})) %all-reduce.3.cloned.1.call-update) | async-done | bytes 524304 | tf_op jit(solution)/shard_map/psum | solution.py:99
  470.5 1.8 convert_element_type.48
  472.3 1.8 convert_element_type.51
  (38 shorter events, 0.5 us)
Async XLA Ops:
  7.2 10.9 %copy-start = (s32[128,1]{0,1:T(1,128)S(1)}, s32[128,1]{0,1:T(1,128)}, u32[]{:S(2)}) copy-start(s32[128,1]{0,1:T(1,128)} %param.12) | copy-start | bytes 1540
  7.2 44.9 %all-gather.9.cloned.1.call-start = ((), (), s32[]{:S(2)}) async-start(), calls=%async_computation.6 | async-start | bytes 2359296 | tf_op jit(solution)/shard_map/all_gather | solution.py:49
  9.0 85.3 %all-gather.11.cloned.1.call-start = ((), (), s32[]{:S(2)}) async-start(), calls=%async_computation.8 | async-start | bytes 2359296 | tf_op jit(solution)/shard_map/all_gather | solution.py:67
  10.9 127.8 %all-gather.7.cloned.1.call-start = ((), (), s32[]{:S(2)}) async-start(), calls=%async_computation.5 | async-start | bytes 4456448 | tf_op jit(solution)/shard_map/all_gather | solution.py:51
  11.7 168.8 %all-gather.5.cloned.1.call-start = ((), (), s32[]{:S(2)}) async-start(), calls=%async_computation.4 | async-start | bytes 4456448 | tf_op jit(solution)/shard_map/all_gather | solution.py:58
  12.2 308.5 %reduce-scatter.9.cloned.1.call-start = ((), (), s32[]{:S(2)}) async-start(), calls=%async_computation.10 | async-start | bytes 4456448 | tf_op jit(solution)/shard_map/reduce_scatter | solution.py:91
  185.7 5.0 %copy-start.2 = (bf16[128,128,128]{2,1,0:T(8,128)(2,1)S(1)}, bf16[128,128,128]{2,1,0:T(8,128)(2,1)}, u32[]{:S(2)}) copy-start(bf16[128,128,128]{2,1,0:T(8,128)(2,1)} %gather_fusion.4) | copy-start | bytes 12582916
  199.2 137.9 %reduce-scatter.11.cloned.1.call-start = ((), (), s32[]{:S(2)}) async-start(), calls=%async_computation.11 | async-start | bytes 4456448 | tf_op jit(solution)/shard_map/reduce_scatter | solution.py:94
  219.4 160.0 %reduce-scatter.7.cloned.1.call-start = ((), (), s32[]{:S(2)}) async-start(), calls=%async_computation.9 | async-start | bytes 2359296 | tf_op jit(solution)/shard_map/reduce_scatter | solution.py:77
  269.9 153.1 %reduce-scatter.5.cloned.1.call-start = ((), (), s32[]{:S(2)}) async-start(), calls=%async_computation.7 | async-start | bytes 2359296 | tf_op jit(solution)/shard_map/reduce_scatter | solution.py:64
  315.1 158.9 %copy-start.1 = (s32[128,1]{0,1:T(1,128)S(1)}, s32[128,1]{0,1:T(1,128)}, u32[]{:S(2)}) copy-start(s32[128,1]{0,1:T(1,128)} %param.12) | copy-start | bytes 1540
  320.7 149.9 %all-reduce.3.cloned.1.call-start = ((), (), s32[]{:S(2)}) async-start(), calls=%async_computation.12 | async-start | bytes 1048576 | tf_op jit(solution)/shard_map/psum | solution.py:99
Sparse Core Ops, SparseCore 0:
  10.4 41.6 all-gather.8
  54.5 39.8 all-gather.10
  96.2 42.5 all-gather.6
  140.4 39.9 all-gather.4
  199.3 66.5 reduce-scatter.8
  268.4 68.6 reduce-scatter.10
  339.7 39.6 reduce-scatter.6
  381.9 41.0 reduce-scatter.4
  425.7 44.8 all-reduce.2
where the time goes:
time: 482 us; the launch traced here: 481 us
  waiting for transfers between devices  279 us (58%)
  local copies, waits for them, and re-layouts  81.1 us (17%)
  other arithmetic  73.8 us (15%)
  matrix products  32.2 us (7%)
  between operations  14 us (3%)
    scatter-add x2, other arithmetic, add_far(): jnp.zeros((rows_here, model_blocks, block_size), jnp.float32)  53.6 us
    psum x1, waiting for transfers between devices, body(): lax.psum(up_part.astype(jnp.bfloat16), 'dp').astype(jnp.float32)  45.7 us
    reduce_scatter x1, waiting for transfers between devices, body(): lax.psum_scatter(partial_in.astype(jnp.bfloat16), 'tensor', scatter_dimen...  42.2 us
    reduce_scatter x1, waiting for transfers between devices, body(): lax.psum_scatter(partial_out.astype(jnp.bfloat16), 'tensor', scatter_dime...  41.9 us
    all_gather x1, waiting for transfers between devices, body(): full_cotangent = lax.all_gather(cotangent, 'tensor', axis=1, tiled=True)  39 us
    all_gather x1, waiting for transfers between devices, body(): up_whole = lax.all_gather(up_tiles, 'fsdp', axis=0, tiled=True)  32.7 us
    all_gather x1, waiting for transfers between devices, body(): down_whole = lax.all_gather(down_tiles, 'fsdp', axis=0, tiled=True)  31.7 us
    all_gather x1, waiting for transfers between devices, body(): full_input = lax.all_gather(activations, 'tensor', axis=1, tiled=True)  28 us
  transfers between devices with their start and end apart: 9, of which 8 were waited for; matrix products, arithmetic and copies ran while one was open for 34% of the time, Pallas kernels for 0%

commit v1 on v0

--- a/solution.py
+++ b/solution.py
@@ -55,7 +55,9 @@
     )
     gelu_out, gelu_slope = gelu_parts(pre_act)
     hidden = gelu_out.astype(jnp.bfloat16)
-    down_whole = lax.all_gather(down_tiles, "fsdp", axis=0, tiled=True)
+    down_whole = jnp.concatenate(
+        lax.all_to_all(jnp.stack([down_tiles] * lax.axis_size("fsdp")), "fsdp", 0, 0), axis=0
+    )
     down_sorted = grouped_tiles(down_whole, down_order, hidden_blocks)
     out_product = jnp.einsum(
         "thb,hkbc->thkc", hidden, down_sorted, preferred_element_type=jnp.float32

time: 482 us -> 445 us (0.923)
  waiting for transfers between devices: 279 us -> 233 us
  starting transfers between devices: 0.55 us -> 8.14 us
  local copies, waits for them, and re-layouts: 81.1 us -> 86.5 us
    all_gather x1 -> x0, waiting for transfers between devices: 31.7 us -> none  [body(): down_whole = lax.all_gather(down_tiles, 'fsdp', axis=0, tiled=True)]
    all_gather x1, waiting for transfers between devices: 28 us -> 20 us  [body(): full_input = lax.all_gather(activations, 'tensor', axis=1, tiled=True)]
    all_to_all x0 -> x1, starting transfers between devices: none -> 7.63 us  [body(): lax.all_to_all(jnp.stack([down_tiles] * lax.axis_size('fsdp')), 'fsdp', 0...]
    all_gather x1, waiting for transfers between devices: 32.7 us -> 27.4 us  [body(): up_whole = lax.all_gather(up_tiles, 'fsdp', axis=0, tiled=True)]
  transfers between devices with their start and end apart: 9 -> 9, of which waited for: 8 -> 7; matrix products, arithmetic and copies ran while one was open for 34% -> 36% of each run, Pallas kernels for 0% -> 0%
where the time goes in v1:
time: 445 us; the launch traced here: 443 us
  waiting for transfers between devices  233 us (52%)
  local copies, waits for them, and re-layouts  86.5 us (19%)
  other arithmetic  72.5 us (16%)
  matrix products  28.7 us (6%)
  between operations  14.3 us (3%)
  starting transfers between devices  8.14 us (2%)
    scatter-add x2, other arithmetic, add_far(): jnp.zeros((rows_here, model_blocks, block_size), jnp.float32)  53.6 us
    psum x1, waiting for transfers between devices, body(): lax.psum(up_part.astype(jnp.bfloat16), 'dp').astype(jnp.float32)  46 us
    reduce_scatter x1, waiting for transfers between devices, body(): lax.psum_scatter(partial_in.astype(jnp.bfloat16), 'tensor', scatter_dimen...  42.2 us
    reduce_scatter x1, waiting for transfers between devices, body(): lax.psum_scatter(partial_out.astype(jnp.bfloat16), 'tensor', scatter_dime...  41.7 us
    all_gather x1, waiting for transfers between devices, body(): full_cotangent = lax.all_gather(cotangent, 'tensor', axis=1, tiled=True)  38.2 us
    all_gather x1, waiting for transfers between devices, body(): up_whole = lax.all_gather(up_tiles, 'fsdp', axis=0, tiled=True)  27.4 us
    all_gather x1, waiting for transfers between devices, body(): full_input = lax.all_gather(activations, 'tensor', axis=1, tiled=True)  20 us
    reshape x2, local copies, waits for them, and re-layouts, add_far(): flat = product.reshape(rows_here, -1, block_size)  18 us
  transfers between devices with their start and end apart: 9, of which 7 were waited for; matrix products, arithmetic and copies ran while one was open for 36% of the time, Pallas kernels for 0%

profile of v1, /device:TPU:1, one launch (start us, length us, event | category | flops | bytes accessed | tf_op | source)
XLA Modules:
  0.0 443.0 jit_solution(12582740605940836150)
XLA Ops:
  7.2 1.8 copy.58
  9.1 1.8 copy.65
  11.7 4.0 stack.2
  15.6 7.6 %all-to-all-start = ((bf16[16,8,128,128]{3,2,1,0:T(8,128)(2,1)}), bf16[16,8,128,128]{3,2,1,0:T(8,128)(2,1)}, u32[]{:S(2)}, u32[]{:S(2)}) async-start(bf16[16,8,128,128]{3,2,1,0:T(8,128)(2,1)} %stack.2), calls=%async_computation | async-start | bytes 8388608 | tf_op jit(solution)/shard_map/all_to_all | solution.py:59
  23.3 2.5 sort.63
  25.9 2.5 sort.64
  28.4 1.2 gather_fusion.3
  29.7 2.5 sort.62
  32.2 1.2 gather_fusion
  33.5 20.0 %all-gather.6.cloned.1.call-done = bf16[128,8192]{0,1:T(8,128)(2,1)} async-done(((bf16[128,1024]{0,1:T(8,128)(2,1)}), bf16[128,8192]{0,1:T(8,128)(2,1)}) %all-gather.6.cloned.1.call-update) | async-done | bytes 2097168 | tf_op jit(solution)/shard_map/all_gather | solution.py:49
  53.5 3.2 copy.59
  56.8 38.2 %all-gather.8.cloned.1.call-done = bf16[128,8192]{0,1:T(8,128)(2,1)} async-done(((bf16[128,1024]{0,1:T(8,128)(2,1)}), bf16[128,8192]{0,1:T(8,128)(2,1)}) %all-gather.8.cloned.1.call-update) | async-done | bytes 2097168 | tf_op jit(solution)/shard_map/all_gather | solution.py:69
  95.0 4.1 copy.66
  99.1 3.0 gather_fusion.4
  102.1 4.6 %gather_fusion.5 = bf16[128,128,128]{2,1,0:T(8,128)(2,1)} fusion(bf16[128,64,128]{2,0,1:T(8,128)(2,1)} %copy.66, s32[1024]{0:T(1024)S(1)} %pad_clamp_fusion.2), kind=kCustom, calls=%fused_computation.5 | custom fusion | bytes 8389120 | tf_op jit(solution)/shard_map/gather | solution.py:20
  106.8 5.2 %gather_fusion.1 = bf16[128,128,128]{2,1,0:T(8,128)(2,1)} fusion(bf16[128,128,128]{2,1,0:T(8,128)(2,1)} %bitcast.4, s32[1024]{0:T(1024)S(1)} %pad_clamp_fusion.5), kind=kCustom, calls=%fused_computation.1 | custom fusion | bytes 8389120 | tf_op jit(solution)/shard_map/gather | solution.py:36
  112.0 27.4 %all-gather.4.cloned.1.call-done = bf16[128,128,128]{2,1,0:T(8,128)(2,1)} async-done(((bf16[8,128,128]{2,1,0:T(8,128)(2,1)}), bf16[128,128,128]{2,1,0:T(8,128)(2,1)}) %all-gather.4.cloned.1.call-update) | async-done | bytes 4194320 | tf_op jit(solution)/shard_map/all_gather | solution.py:51
  139.4 5.2 %gather_fusion.2 = bf16[128,128,128]{2,1,0:T(8,128)(2,1)} fusion(bf16[128,128,128]{2,1,0:T(8,128)(2,1)} %all-gather.4.cloned.1.call-done, s32[1024]{0:T(1024)S(1)} %pad_clamp_fusion.4), kind=kCustom, calls=%fused_computation.2 | custom fusion | bytes 8389120 | tf_op jit(solution)/shard_map/gather | solution.py:36
  144.6 4.9 %convolution_bitcast_fusion.1 = f32[128,16,128]{0,2,1:T(8,128)S(1)} fusion(bf16[16,8,128,128]{3,2,1,0:T(8,128)(2,1)} %bitcast.77, bf16[128,16,8,128]{3,0,2,1:T(8,128)(2,1)} %bitcast.79), kind=kOutput, calls=%fused_computation.14 | convolution fusion | flops 536870912 | bytes 9437184 | tf_op jit(solution)/shard_map/thkb,hkbc->thc/dot_general | solution.py:53
  149.6 1.0 copy-done.5
  150.6 1.3 fusion.2
  151.9 0.8 copy-done.3
  152.7 3.3 convolution_convert_fusion.1
  156.1 5.2 %gather_fusion.6 = bf16[128,128,128]{2,1,0:T(8,128)(2,1)} fusion(bf16[128,128,128]{2,1,0:T(8,128)(2,1)} %bitcast.89, s32[1024]{0:T(1024)S(1)} %pad_clamp_fusion.1), kind=kCustom, calls=%fused_computation.6 | custom fusion | bytes 8389120 | tf_op jit(solution)/shard_map/gather | solution.py:90
  161.5 2.5 sort.65
  164.1 5.6 %convolution_convert_fusion = bf16[16,8,128,128]{3,2,1,0:T(8,128)(2,1)} fusion(bf16[128,16,8,128]{3,0,2,1:T(8,128)(2,1)} %bitcast.87, f32[128,16,128]{0,2,1:T(8,128)S(1)} %convolution_bitcast_fusion.1), kind=kOutput, calls=%fused_computation.10 | convolution fusion | flops 540278784 | bytes 9437184 | tf_op jit(solution)/shard_map/thb,thkc->hkbc/dot_general | solution.py:85
  169.7 6.4 %copy.74 = bf16[128,128,128]{2,1,0:T(8,128)(2,1)} copy(bf16[128,128,128]{1,2,0:T(8,128)(2,1)} %bitcast.90) | data formatting | bytes 8388608 | tf_op jit(solution)/shard_map/reshape | solution.py:89
  176.1 5.3 %gather_fusion.7 = bf16[128,128,128]{2,1,0:T(8,128)(2,1)} fusion(bf16[128,128,128]{2,1,0:T(8,128)(2,1)} %copy.74, s32[1024]{0:T(1024)S(1)} %pad_clamp_fusion), kind=kCustom, calls=%fused_computation.7 | custom fusion | bytes 8389120 | tf_op jit(solution)/shard_map/gather | solution.py:91
  181.4 6.7 %fusion.13 = f32[16,8,128,128]{3,2,1,0:T(8,128)} fusion(bf16[16,8,128,128]{3,2,1,0:T(8,128)(2,1)} %bitcast.78, bf16[128,16,128,1]{0,2,3,1:T(8,128)(2,1)S(1)} %fusion.2), kind=kOutput, calls=%fused_computation.40 | convolution fusion | flops 536870912 | bytes 13107200 | tf_op jit(solution)/shard_map/thc,hkbc->thkb/dot_general | solution.py:75
  188.2 9.0 %copy.68 = f32[128,128,128]{2,0,1:T(8,128)} copy(f32[128,128,128]{0,2,1:T(8,128)} %bitcast.83) | data formatting | bytes 16777216 | tf_op jit(solution)/shard_map/reshape | solution.py:27
  197.2 2.5 broadcast.44.clone.1
  199.7 26.7 %scatter_fusion.1 = f32[128,64,128]{2,0,1:T(8,128)} fusion(f32[128,64,128]{2,0,1:T(8,128)} %broadcast.44.clone.1, s32[128]{0:T(128)S(1)} %fusion.9, f32[128,128,128]{2,1,0:T(8,128)} %bitcast.82), kind=kCustom, calls=%fused_computation.9 | custom fusion | flops 2097152 | bytes 25166336 | tf_op jit(solution)/shard_map/scatter-add | solution.py:29
  226.3 2.6 convert_element_type.45
  229.0 2.9 copy.69
  232.0 6.8 %fusion.11 = f32[16,8,128,128]{3,2,1,0:T(8,128)} fusion(bf16[16,8,128,128]{3,2,1,0:T(8,128)(2,1)} %bitcast.85, f32[128,16,128]{0,2,1:T(8,128)S(1)} %convolution_bitcast_fusion.1), kind=kOutput, calls=%fused_computation.39 | convolution fusion | flops 538181632 | bytes 13631488 | tf_op jit(solution)/shard_map/thb,hkbc->thkc/dot_general | solution.py:62
  238.8 9.0 %copy.63 = f32[128,128,128]{2,0,1:T(8,128)} copy(f32[128,128,128]{0,2,1:T(8,128)} %bitcast.84) | data formatting | bytes 16777216 | tf_op jit(solution)/shard_map/reshape | solution.py:27
  247.8 2.5 broadcast.44.clone
  250.3 26.9 %scatter_fusion = f32[128,64,128]{2,0,1:T(8,128)} fusion(f32[128,64,128]{2,0,1:T(8,128)} %broadcast.44.clone, s32[128]{0:T(128)S(1)} %fusion.8, f32[128,128,128]{2,1,0:T(8,128)} %bitcast.81), kind=kCustom, calls=%fused_computation.8 | custom fusion | flops 2097152 | bytes 25166336 | tf_op jit(solution)/shard_map/scatter-add | solution.py:29
  277.2 2.6 convert_element_type.42
  279.8 2.9 copy.64
  282.8 16.4 %reduce-scatter.11.cloned.1.call-done = bf16[8,128,128]{2,1,0:T(8,128)(2,1)} async-done(((bf16[128,128,128]{2,1,0:T(8,128)(2,1)}), bf16[8,128,128]{2,1,0:T(8,128)(2,1)}) %reduce-scatter.11.cloned.1.call-update) | async-done | bytes 262160 | tf_op jit(solution)/shard_map/reduce_scatter | solution.py:96
  299.2 42.2 %reduce-scatter.7.cloned.1.call-done = bf16[128,1024]{0,1:T(8,128)(2,1)} async-done(((bf16[128,8192]{0,1:T(8,128)(2,1)}), bf16[128,1024]{0,1:T(8,128)(2,1)}) %reduce-scatter.7.cloned.1.call-update) | async-done | bytes 262160 | tf_op jit(solution)/shard_map/reduce_scatter | solution.py:79
  341.3 1.8 copy.76
  343.1 41.7 %reduce-scatter.5.cloned.1.call-done = bf16[128,1024]{0,1:T(8,128)(2,1)} async-done(((bf16[128,8192]{0,1:T(8,128)(2,1)}), bf16[128,1024]{0,1:T(8,128)(2,1)}) %reduce-scatter.5.cloned.1.call-update) | async-done | bytes 262160 | tf_op jit(solution)/shard_map/reduce_scatter | solution.py:66
  384.8 1.8 copy.75
  386.6 46.0 %all-reduce.3.cloned.1.call-done = (bf16[8,128,128]{2,1,0:T(8,128)(2,1)}, bf16[8,128,128]{2,1,0:T(8,128)(2,1)}) async-done(((bf16[8,128,128]{2,1,0:T(8,128)(2,1)}, bf16[8,128,128]{2,1,0:T(8,128)(2,1)}), (bf16[8,128,128]{2,1,0:T(8,128)(2,1)}, bf16[8,128,128]{2,1,0:T(8,128)(2,1)})) %all-reduce.3.cloned.1.call-update) | async-done | bytes 524304 | tf_op jit(solution)/shard_map/psum | solution.py:101
  432.6 1.8 convert_element_type.48
  434.4 1.8 convert_element_type.51
  (48 shorter events, 1.4 us)
Async XLA Ops:
  7.2 21.2 %copy-start = (s32[128,1]{0,1:T(1,128)S(1)}, s32[128,1]{0,1:T(1,128)}, u32[]{:S(2)}) copy-start(s32[128,1]{0,1:T(1,128)} %param.12) | copy-start | bytes 1540
  7.2 46.4 %all-gather.6.cloned.1.call-start = ((), (), s32[]{:S(2)}) async-start(), calls=%async_computation.6 | async-start | bytes 2359296 | tf_op jit(solution)/shard_map/all_gather | solution.py:49
  9.0 86.0 %all-gather.8.cloned.1.call-start = ((), (), s32[]{:S(2)}) async-start(), calls=%async_computation.8 | async-start | bytes 2359296 | tf_op jit(solution)/shard_map/all_gather | solution.py:69
  10.9 128.5 %all-gather.4.cloned.1.call-start = ((), (), s32[]{:S(2)}) async-start(), calls=%async_computation.5 | async-start | bytes 4456448 | tf_op jit(solution)/shard_map/all_gather | solution.py:51
  15.6 7.7 %copy-start.6 = (s32[128,1]{0,1:T(1,128)S(1)}, s32[128,1]{0,1:T(1,128)}, u32[]{:S(2)}) copy-start(s32[128,1]{0,1:T(1,128)} %param.13) | copy-start | bytes 1540
  15.6 14.0 %copy-start.7 = (s32[128,1]{0,1:T(1,128)S(1)}, s32[128,1]{0,1:T(1,128)}, u32[]{:S(2)}) copy-start(s32[128,1]{0,1:T(1,128)} %param.14) | copy-start | bytes 1540
  15.6 16.6 %copy-start.2 = (s32[128,1]{0,1:T(1,128)S(1)}, s32[128,1]{0,1:T(1,128)}, u32[]{:S(2)}) copy-start(s32[128,1]{0,1:T(1,128)} %param.15) | copy-start | bytes 1540
  15.6 91.1 %all-to-all-start = ((bf16[16,8,128,128]{3,2,1,0:T(8,128)(2,1)}), bf16[16,8,128,128]{3,2,1,0:T(8,128)(2,1)}, u32[]{:S(2)}, u32[]{:S(2)}) async-start(bf16[16,8,128,128]{3,2,1,0:T(8,128)(2,1)} %stack.2), calls=%async_computation | async-start | bytes 8388608 | tf_op jit(solution)/shard_map/all_to_all | solution.py:59
  23.3 259.5 %reduce-scatter.9.cloned.1.call-start = ((), (), s32[]{:S(2)}) async-start(), calls=%async_computation.10 | async-start | bytes 4456448 | tf_op jit(solution)/shard_map/reduce_scatter | solution.py:93
  144.6 4.9 %copy-start.4 = (bf16[128,128,128]{2,1,0:T(8,128)(2,1)S(1)}, bf16[128,128,128]{2,1,0:T(8,128)(2,1)}, u32[]{:S(2)}) copy-start(bf16[128,128,128]{2,1,0:T(8,128)(2,1)} %gather_fusion.1) | copy-start | bytes 12582916
  144.6 5.9 %copy-start.5 = (bf16[128,128,128]{2,1,0:T(8,128)(2,1)S(1)}, bf16[128,128,128]{2,1,0:T(8,128)(2,1)}, u32[]{:S(2)}) copy-start(bf16[128,128,128]{2,1,0:T(8,128)(2,1)} %gather_fusion.5) | copy-start | bytes 12582916
  150.5 2.2 copy-start.3
  161.3 137.8 %reduce-scatter.11.cloned.1.call-start = ((), (), s32[]{:S(2)}) async-start(), calls=%async_computation.11 | async-start | bytes 4456448 | tf_op jit(solution)/shard_map/reduce_scatter | solution.py:96
  181.4 159.9 %reduce-scatter.7.cloned.1.call-start = ((), (), s32[]{:S(2)}) async-start(), calls=%async_computation.9 | async-start | bytes 2359296 | tf_op jit(solution)/shard_map/reduce_scatter | solution.py:79
  232.0 152.9 %reduce-scatter.5.cloned.1.call-start = ((), (), s32[]{:S(2)}) async-start(), calls=%async_computation.7 | async-start | bytes 2359296 | tf_op jit(solution)/shard_map/reduce_scatter | solution.py:66
  277.2 159.0 %copy-start.1 = (s32[128,1]{0,1:T(1,128)S(1)}, s32[128,1]{0,1:T(1,128)}, u32[]{:S(2)}) copy-start(s32[128,1]{0,1:T(1,128)} %param.12) | copy-start | bytes 1540
  282.7 149.9 %all-reduce.3.cloned.1.call-start = ((), (), s32[]{:S(2)}) async-start(), calls=%async_computation.12 | async-start | bytes 1048576 | tf_op jit(solution)/shard_map/psum | solution.py:101
Sparse Core Ops, SparseCore 0:
  10.4 43.1 all-gather.5
  55.9 39.0 all-gather.7
  96.9 42.5 all-gather.3
  161.4 66.6 reduce-scatter.8
  230.5 68.6 reduce-scatter.10
  301.5 39.7 reduce-scatter.6
  343.9 40.8 reduce-scatter.4
  387.4 45.1 all-reduce.2
